TPU v7x, 128 devices: a whole 4x4x4 slice. The times are simulated.
128 devices in a mesh: dp: 32 (over y, x, core), chan: 4 (over z).
Axes of the slice: x: 4, y: 4, z: 4, core: 2. Of those that a mesh axis runs over, the one named last changes fastest.
Arguments:
- activations: bfloat16 [256, 32, 32, 512], P('dp'), may hold values from -12 to 12
- out_grads: bfloat16 [256, 32, 32, 512], P('dp', None, None, 'chan'), may hold values from -4 to 4
- weight: float32 [512, 3, 3, 512], P('dp', None, None, 'chan'), may hold values from -6 to 6
- momentum: float32 [512, 3, 3, 512], P('dp', None, None, 'chan'), may hold values from -6 to 6
Outputs:
- new_weight: float32 [512, 3, 3, 512], P('dp', None, None, 'chan')
- new_momentum: float32 [512, 3, 3, 512], P('dp', None, None, 'chan')
All inputs are finite; a program needn't handle non-finite values.
Results may differ from a plain program's by a relative error of at most 0.0003.
Values sent between devices are 32-bit elements; how exact they have to be, the bound alone decides.
A program may use at most 64 MiB of HBM per device.

v0:
```python
import jax
import jax.numpy as jnp
from jax import lax
from jax.sharding import PartitionSpec as P

HEIGHT = 32
BREADTH = 32


def partner(block, axis, apart):
    count = lax.axis_size(axis)
    route = []
    for low in range(count):
        high = low | 1 << apart
        if high != low and high < count:
            route += [(low, high), (high, low)]
    return lax.ppermute(block, axis, route)


def local_gradient(activations, out_grads):
    padded = jnp.pad(activations, ((0, 0), (1, 1), (1, 1), (0, 0)))
    outputs = []
    for row_off in range(3):
        for col_off in range(3):
            window = padded[:, row_off : row_off + HEIGHT, col_off : col_off + BREADTH, :]
            outputs.append(
                jnp.einsum("bhwc,bhwo->co", window, out_grads, preferred_element_type=jnp.float32)
            )
    stacked = jnp.stack(outputs, axis=1)
    return stacked.reshape(activations.shape[3], 3, 3, out_grads.shape[3])


def pair_partials(lower_vec, upper_vec):
    return jnp.stack(
        [
            jnp.sum(lower_vec * upper_vec),
            jnp.sum(lower_vec * lower_vec),
            jnp.sum(upper_vec * upper_vec),
        ]
    )


def apply_combine(lower_vec, upper_vec, sums):
    lower_coef = 1.0 - sums[0] / (2.0 * (sums[1] + 1e-06))
    upper_coef = 1.0 - sums[0] / (2.0 * (sums[2] + 1e-06))
    return lower_coef * lower_vec + upper_coef * upper_vec


def shards(activations, out_grads, weight, momentum):
    gradient = local_gradient(activations, out_grads)
    ndevices = lax.axis_size("dp")
    levels_count = ndevices.bit_length() - 1
    my_index = lax.axis_index("dp")
    in_rows = gradient.shape[0]
    portion = gradient.reshape((ndevices, in_rows // ndevices) + gradient.shape[1:])
    for level_idx in range(levels_count):
        count = portion.shape[0]
        paired = portion.reshape((count // 2, 2) + portion.shape[1:])
        my_bit = my_index >> level_idx & 1
        is_lower = my_bit == 0
        kept_part = jnp.where(is_lower, paired[:, 0], paired[:, 1])
        sent_part = jnp.where(is_lower, paired[:, 1], paired[:, 0])
        received = partner(sent_part, "dp", level_idx)
        lower_vec = jnp.where(is_lower, kept_part, received)
        upper_vec = jnp.where(is_lower, received, kept_part)
        partials = pair_partials(lower_vec, upper_vec)
        groups = ndevices >> level_idx + 1
        group_id = my_index >> level_idx + 1
        group_mask = (jnp.arange(groups) == group_id).astype(jnp.float32)
        slots = group_mask[:, None] * partials[None, :]
        summed = lax.psum(slots, ("dp", "chan"))
        sums = jnp.sum(group_mask[:, None] * summed, axis=0)
        portion = apply_combine(lower_vec, upper_vec, sums)
    result = portion[0]
    new_momentum = 0.9 * momentum + result
    new_weight = weight - 0.1 * new_momentum
    return (new_weight, new_momentum)


def solution(mesh):
    in_specs = (
        P("dp", None, None, None),
        P("dp", None, None, "chan"),
        P("dp", None, None, "chan"),
        P("dp", None, None, "chan"),
    )
    out_specs = (P("dp", None, None, "chan"), P("dp", None, None, "chan"))
    return jax.shard_map(shards, mesh=mesh, in_specs=in_specs, out_specs=out_specs, check_vma=False)
```

profile of v0, /device:TPU:1, one launch (start us, length us, event | category | flops | bytes accessed | tf_op | source)
XLA Modules:
  0.0 430.9 jit_solution(7475140483685385099)
XLA Ops:
  0.6 0.0 copy-start
  0.7 1.6 copy-done
  2.2 0.0 copy-start.4
  2.2 5.1 %fusion.23 = f32[512,9,128]{2,0,1:T(8,128)S(1)} fusion(bf16[8,32,32,128]{3,2,1,0:T(8,128)(2,1)S(1)} %copy-done, bf16[8,32,32,512]{3,2,1,0:T(8,128)(2,1)} %param.4), kind=kOutput, calls=%fused_computation.38 | convolution fusion | flops 1073741824 | bytes 10747904 | tf_op jit(solution)/shard_map/bhwc,bhwo->co/dot_general | solution.py:27
  7.4 0.6 copy-done.4
  8.0 2.4 fusion.21
  10.5 2.4 fusion.19
  12.9 2.4 fusion.17
  15.4 2.4 fusion.24
  17.8 2.6 fusion.15
  20.4 2.5 fusion.13
  22.9 2.4 fusion.11
  25.3 2.5 fusion.9
  27.8 0.2 fusion.36
  27.9 0.0 copy-start.1
  27.9 1.0 copy-done.1
  28.9 1.2 select_bitcast_fusion
  30.1 1.4 collective-permute-start
  31.6 2.8 collective-permute-done
  34.4 4.0 multiply_reduce_fusion.2
  38.4 1.9 pad_maximum_fusion
  40.3 0.1 broadcast_multiply_fusion.2
  40.4 67.9 %psum.35 = f32[16,3]{0,1:T(4,128)S(1)} all-reduce(f32[16,3]{0,1:T(4,128)S(1)} %broadcast_multiply_fusion.2), channel_id=1, replica_groups=mesh['dp'=32,'chan'=4] {'dp','chan'}, use_global_device_ids=true, to_apply=%region_3.4 | all-reduce | flops 48 | bytes 384 | tf_op jit(solution)/shard_map/psum | solution.py:71
  108.3 0.1 multiply_reduce_fusion.17
  108.4 0.7 fusion.41
  111.7 1.8 multiply_add_fusion
  113.5 0.9 select_bitcast_fusion.1
  114.4 0.0 collective-permute-start.1
  114.4 14.3 %collective-permute-done.1 = f32[8,16,3,3,128]{4,1,3,2,0:T(8,128)} collective-permute-done((f32[8,16,3,3,128]{4,1,3,2,0:T(8,128)}, f32[8,16,3,3,128]{4,1,3,2,0:T(8,128)}, u32[]{:S(2)}, u32[]{:S(2)}) %collective-permute-start.1) | collective-permute-done | bytes 589856 | tf_op jit(solution)/shard_map/ppermute | solution.py:17
  128.7 2.9 multiply_reduce_fusion.5
  131.6 2.0 pad_maximum_fusion.1
  133.6 0.1 broadcast_multiply_fusion.1
  133.7 63.4 %psum.36 = f32[8,3]{0,1:T(4,128)S(1)} all-reduce(f32[8,3]{0,1:T(4,128)S(1)} %broadcast_multiply_fusion.1), channel_id=1, replica_groups=mesh['dp'=32,'chan'=4] {'dp','chan'}, use_global_device_ids=true, to_apply=%region_8.9 | all-reduce | flops 24 | bytes 192 | tf_op jit(solution)/shard_map/psum | solution.py:71
  197.0 0.1 multiply_reduce_fusion.16
  197.2 0.6 fusion.40
  200.3 1.3 multiply_add_fusion.1
  201.7 1.8 collective-permute-start.2
  203.5 0.0 copy-start.2
  203.5 0.0 copy-start.3
  203.5 8.1 %collective-permute-done.2 = f32[4,16,3,3,128]{4,1,3,2,0:T(8,128)} collective-permute-done((f32[4,16,3,3,128]{4,1,3,2,0:T(8,128)S(1)}, f32[4,16,3,3,128]{4,1,3,2,0:T(8,128)}, u32[]{:S(2)}, u32[]{:S(2)}) %collective-permute-start.2) | collective-permute-done | bytes 294944 | tf_op jit(solution)/shard_map/ppermute | solution.py:17
  211.5 1.7 multiply_reduce_fusion.8
  213.2 1.9 pad_maximum_fusion.2
  215.1 0.1 broadcast_multiply_fusion
  215.2 63.1 %psum.37 = f32[4,3]{1,0:T(4,128)S(1)} all-reduce(f32[4,3]{1,0:T(4,128)S(1)} %broadcast_multiply_fusion), channel_id=1, replica_groups=mesh['dp'=32,'chan'=4] {'dp','chan'}, use_global_device_ids=true, to_apply=%region_13.14 | all-reduce | flops 12 | bytes 96 | tf_op jit(solution)/shard_map/psum | solution.py:71
  278.3 0.1 multiply_reduce_fusion.15
  278.3 0.7 fusion.39
  281.8 0.1 collective-permute-start.3
  281.9 4.7 %collective-permute-done.3 = f32[2,16,3,3,128]{4,1,3,2,0:T(8,128)S(1)} collective-permute-done((f32[2,16,3,3,128]{4,1,3,2,0:T(8,128)S(1)}, f32[2,16,3,3,128]{4,1,3,2,0:T(8,128)S(1)}, u32[]{:S(2)}, u32[]{:S(2)}) %collective-permute-start.3) | collective-permute-done | bytes 147488 | tf_op jit(solution)/shard_map/ppermute | solution.py:17
  286.6 0.8 multiply_reduce_fusion.11
  287.4 2.1 pad_maximum_fusion.3
  289.4 0.1 broadcast_multiply_fusion.3
  289.5 63.1 %psum.38 = f32[2,3]{1,0:T(2,128)S(1)} all-reduce(f32[2,3]{1,0:T(2,128)S(1)} %broadcast_multiply_fusion.3), channel_id=1, replica_groups=mesh['dp'=32,'chan'=4] {'dp','chan'}, use_global_device_ids=true, to_apply=%region_18.19 | all-reduce | flops 6 | bytes 48 | tf_op jit(solution)/shard_map/psum | solution.py:71
  352.6 0.1 multiply_reduce_fusion.18
  352.7 0.7 fusion.38
  356.1 1.4 collective-permute-start.4
  357.5 3.4 collective-permute-done.4
  360.9 0.7 multiply_reduce_fusion.14
  361.6 2.1 maximum_multiply_fusion
  363.7 63.1 %psum.39 = f32[1,3]{1,0:T(1,128)S(1)} all-reduce(f32[1,3]{1,0:T(1,128)S(1)} %maximum_multiply_fusion), channel_id=1, replica_groups=mesh['dp'=32,'chan'=4] {'dp','chan'}, use_global_device_ids=true, to_apply=%region_23.24 | all-reduce | flops 3 | bytes 24 | tf_op jit(solution)/shard_map/psum | solution.py:71
  426.8 0.7 fusion.37
  430.2 0.0 copy-done.2
  430.2 0.0 copy-done.3
  430.2 0.7 multiply_subtract_fusion
  (10 shorter events, 0.1 us)
Async XLA Ops:
  0.6 1.6 copy-start
  2.2 5.8 %copy-start.4 = (bf16[8,32,32,512]{3,2,1,0:T(8,128)(2,1)S(1)}, bf16[8,32,32,512]{3,2,1,0:T(8,128)(2,1)}, u32[]{:S(2)}) copy-start(bf16[8,32,32,512]{3,2,1,0:T(8,128)(2,1)} %param.4) | copy-start | bytes 25165828
  27.9 1.0 copy-start.1
  30.1 4.2 collective-permute-start
  114.4 14.3 %collective-permute-start.1 = (f32[8,16,3,3,128]{4,1,3,2,0:T(8,128)}, f32[8,16,3,3,128]{4,1,3,2,0:T(8,128)}, u32[]{:S(2)}, u32[]{:S(2)}) collective-permute-start(f32[8,16,3,3,128]{4,1,3,2,0:T(8,128)} %select_bitcast_fusion.1), channel_id=1, source_target_pairs={{0,8},{8,0},{4,12},{12,4},{16,24},{24,16},{20,28},{28,20},{32,40},... | collective-permute-start | bytes 1769480 | tf_op jit(solution)/shard_map/ppermute | solution.py:17
  201.7 9.8 %collective-permute-start.2 = (f32[4,16,3,3,128]{4,1,3,2,0:T(8,128)S(1)}, f32[4,16,3,3,128]{4,1,3,2,0:T(8,128)}, u32[]{:S(2)}, u32[]{:S(2)}) collective-permute-start(f32[4,16,3,3,128]{4,1,3,2,0:T(8,128)S(1)} %select_bitcast_fusion.2), channel_id=1, source_target_pairs={{0,16},{16,0},{4,20},{20,4},{8,24},{24,8},{12,28},{28,12},{32,48},... | collective-permute-start | bytes 884744 | tf_op jit(solution)/shard_map/ppermute | solution.py:17
  203.5 226.7 %copy-start.2 = (f32[16,3,3,128]{3,0,2,1:T(8,128)S(1)}, f32[16,3,3,128]{3,0,2,1:T(8,128)}, u32[]{:S(2)}) copy-start(f32[16,3,3,128]{3,0,2,1:T(8,128)} %param.6) | copy-start | bytes 221188
  203.5 226.7 %copy-start.3 = (f32[16,3,3,128]{3,0,2,1:T(8,128)S(1)}, f32[16,3,3,128]{3,0,2,1:T(8,128)}, u32[]{:S(2)}) copy-start(f32[16,3,3,128]{3,0,2,1:T(8,128)} %param.7) | copy-start | bytes 221188
  281.8 4.8 %collective-permute-start.3 = (f32[2,16,3,3,128]{4,1,3,2,0:T(8,128)S(1)}, f32[2,16,3,3,128]{4,1,3,2,0:T(8,128)S(1)}, u32[]{:S(2)}, u32[]{:S(2)}) collective-permute-start(f32[2,16,3,3,128]{4,1,3,2,0:T(8,128)S(1)} %select_bitcast_fusion.3), channel_id=1, source_target_pairs={{0,32},{32,0},{4,36},{36,4},{8,40},{40,8},{12,44},{44,12},{16,48},... | collective-permute-start | bytes 442376 | tf_op jit(solution)/shard_map/ppermute | solution.py:17
  356.1 4.8 %collective-permute-start.4 = (f32[1,16,3,3,128]{4,1,3,2,0:T(8,128)S(1)}, f32[1,16,3,3,128]{4,1,3,2,0:T(8,128)S(1)}, u32[]{:S(2)}, u32[]{:S(2)}) collective-permute-start(f32[1,16,3,3,128]{4,1,3,2,0:T(8,128)S(1)} %select_bitcast_fusion.4), channel_id=1, source_target_pairs={{0,64},{64,0},{4,68},{68,4},{8,72},{72,8},{12,76},{76,12},{16,80},... | collective-permute-start | bytes 221192 | tf_op jit(solution)/shard_map/ppermute | solution.py:17
where the time goes:
time: 432 us; the launch traced here: 431 us
  blocking collectives  321 us (74%)
  waiting for transfers between devices  33.3 us (8%)
  other arithmetic  26.6 us (6%)
  matrix products  24.9 us (6%)
  between operations  14.1 us (3%)
  local copies, waits for them, and re-layouts  6.67 us (2%)
  starting transfers between devices  4.66 us (1%)
    psum x5, blocking collectives, shards(): summed = lax.psum(slots, ('dp', 'chan'))  321 us
    ppermute x5, waiting for transfers between devices, partner(): return lax.ppermute(block, axis, route)  33.3 us
    dot_general x9, matrix products, local_gradient(): jnp.einsum('bhwc,bhwo->co', window, out_grads, preferred_element_type=jnp...  24.9 us
    reduce_sum x5, other arithmetic, pair_partials(): jnp.sum(lower_vec * upper_vec)  9.99 us
  transfers between devices with their start and end apart: 5, of which 5 were waited for; matrix products, arithmetic and copies ran while one was open for 0% of the time, Pallas kernels for 0%

commit v1 on v0

v1 whole, which is shorter than its diff:
```python
import jax
import jax.numpy as jnp
from jax import lax
from jax.experimental import pallas as pl
from jax.experimental.pallas import tpu as pltpu
from jax.sharding import PartitionSpec as P

MESH = pl.DeviceIdType.MESH
SIDE = 4
CHIPS = SIDE * SIDE
DEPTH = 4
ROWS = 16
LANES = 128
SAMPLES = 8
SPACE = 1024
CIN = 512
GROUPS = ((0, 4), (4, 9))
F32 = jnp.float32
EPS = 1e-6


def fold(block):
    halves = block[:, :8] + block[:, 8:]
    return jnp.sum(halves, axis=0)


def total(part):
    return jnp.sum(jnp.sum(part, axis=0, keepdims=True), axis=1, keepdims=True)


def shifted(sample):
    wide = sample.astype(F32)
    column = lax.broadcasted_iota(jnp.int32, wide.shape, 0) % 32
    left = jnp.where(column == 31, 0.0, pltpu.roll(wide, SPACE - 1, 0))
    right = jnp.where(column == 0, 0.0, pltpu.roll(wide, 1, 0))
    return left.astype(sample.dtype), sample, right.astype(sample.dtype)


def pair_weights(gram):
    row = lax.broadcasted_iota(jnp.int32, gram.shape, 0)
    col = lax.broadcasted_iota(jnp.int32, gram.shape, 1)
    weights = jnp.ones((CHIPS, 1), F32)
    size = 1
    while size < CHIPS:
        mine = row // size == col // size
        other = jnp.logical_and(row // (2 * size) == col // (2 * size), jnp.logical_not(mine))
        mask = mine.astype(F32)
        own = gram * mask
        cross = gram * other.astype(F32)
        own_c = jnp.sum(own, axis=0, keepdims=True)
        cross_c = jnp.sum(cross, axis=0, keepdims=True)
        own_r = jnp.sum(own, axis=1, keepdims=True)
        cross_r = jnp.sum(cross, axis=1, keepdims=True)
        square_r = jnp.sum(mask * own_c, axis=1, keepdims=True)
        inner_r = jnp.sum(mask * cross_c, axis=1, keepdims=True)
        square_c = jnp.sum(mask * own_r, axis=0, keepdims=True)
        inner_c = jnp.sum(mask * cross_r, axis=0, keepdims=True)
        coef_r = 1.0 - inner_r / (2.0 * (jnp.maximum(square_r, 0.0) + EPS))
        coef_c = 1.0 - inner_c / (2.0 * (jnp.maximum(square_c, 0.0) + EPS))
        gram = gram * coef_r * coef_c
        weights = weights * coef_r
        size *= 2
    return weights


def kernel(act_hbm, og_hbm, out_ref, act, og, pad, *rest):
    ngroups = len(GROUPS)
    grads, sibs, combs, recvs = (rest[ngroups * i : ngroups * (i + 1)] for i in range(4))
    (scal_src, scal, pairs, gram_src, gram_near, gram_mid, gram_far,
     load_sem, og_sem, sib_send, sib_recv, scal_send, scal_recv, comb_send, comb_recv,
     near_send, near_recv, far_send, far_recv) = rest[4 * ngroups :]

    dp = lax.axis_index("dp")
    z = lax.axis_index("chan")
    chip = dp // 2
    core = dp % 2
    y = chip // SIDE
    x = chip % SIDE
    slot = core * DEPTH + z

    def across(step):
        return (y + step // SIDE) % SIDE * SIDE + (x + step % SIDE) % SIDE

    def near(step):
        return (core + step // DEPTH) % 2, (z + step % DEPTH) % DEPTH

    for b in range(SAMPLES):
        pltpu.make_async_copy(act_hbm.at[b], act.at[b], load_sem.at[b]).start()
        pltpu.make_async_copy(og_hbm.at[b], og.at[b], og_sem.at[b]).start()

    barrier = pltpu.get_barrier_semaphore()

    def greet_far(step, carry):
        pl.semaphore_signal(barrier, inc=1, device_id={"dp": across(step) * 2 + core}, device_id_type=MESH)
        return carry

    def greet_near(step, carry):
        c2, z2 = near(step)
        pl.semaphore_signal(barrier, inc=1, device_id={"dp": chip * 2 + c2, "chan": z2}, device_id_type=MESH)
        return carry

    lax.fori_loop(1, CHIPS, greet_far, 0)
    lax.fori_loop(1, 2 * DEPTH, greet_near, 0)

    for g in grads:
        g[...] = jnp.zeros_like(g)
    pad[...] = jnp.zeros_like(pad)

    def accumulate(b, carry):
        pltpu.make_async_copy(act_hbm.at[b], act.at[b], load_sem.at[b]).wait()
        pltpu.make_async_copy(og_hbm.at[b], og.at[b], og_sem.at[b]).wait()
        for j, moved in enumerate(shifted(og[b])):
            pad[j, 32 : 32 + SPACE, :] = moved
        taps = jnp.concatenate(
            [pad[j, (2 - i) * 32 : (2 - i) * 32 + SPACE, :] for i in range(3) for j in range(3)], axis=1
        )
        product = lax.dot_general(act[b], taps, (((0,), (0,)), ((), ())), preferred_element_type=F32)
        for (first, last), g in zip(GROUPS, grads):
            for t in range(first, last):
                tap = product[:, t * LANES : (t + 1) * LANES].reshape(CHIPS, 2, ROWS, LANES)
                for half in range(2):
                    g[half, :, t - first] += tap[:, half]
        return carry

    lax.fori_loop(0, SAMPLES, accumulate, 0)

    pl.semaphore_wait(barrier, CHIPS - 1 + 2 * DEPTH - 1)

    swaps = []
    for n in range(ngroups):
        swap = pltpu.make_async_remote_copy(
            src_ref=grads[n].at[1 - core],
            dst_ref=sibs[n],
            send_sem=sib_send.at[n],
            recv_sem=sib_recv.at[n],
            device_id={"dp": chip * 2 + 1 - core},
            device_id_type=MESH,
        )
        swap.start()
        swaps.append(swap)
    zero = jnp.zeros((8, LANES), F32)
    sums = (zero, zero, zero)
    for n in range(ngroups):
        swaps[n].wait_recv()

        def products(q, carry, n=n):
            mine = grads[n][core, q]
            theirs = sibs[n][q]
            return (
                carry[0] + fold(mine * theirs),
                carry[1] + fold(mine * mine),
                carry[2] + fold(theirs * theirs),
            )

        sums = lax.fori_loop(0, CHIPS, products, sums)
    scal_src[0] = sums[0]
    scal_src[1] = jnp.where(core == 0, sums[1], sums[2])
    scal_src[2] = jnp.where(core == 0, sums[2], sums[1])
    scal[slot] = scal_src[...]

    def scal_copy(step):
        c2, z2 = near(step)
        return pltpu.make_async_remote_copy(
            src_ref=scal_src,
            dst_ref=scal.at[slot],
            send_sem=scal_send.at[step],
            recv_sem=scal_recv.at[slot],
            device_id={"dp": chip * 2 + c2, "chan": z2},
            device_id_type=MESH,
        )

    def near_wait(step, buffer, sem):
        c2, z2 = near(step)
        s2 = c2 * DEPTH + z2
        pltpu.make_async_copy(buffer.at[s2], buffer.at[s2], sem.at[s2]).wait()

    def start_scal(step, carry):
        scal_copy(step).start()
        return carry

    def wait_scal(step, carry):
        near_wait(step, scal, scal_recv)
        return carry

    lax.fori_loop(1, 2 * DEPTH, start_scal, 0)
    lax.fori_loop(1, 2 * DEPTH, wait_scal, 0)
    added = jnp.sum(scal[...], axis=0)
    inner, low_sq, high_sq = total(added[0]), total(added[1]), total(added[2])
    low = 1.0 - inner / (2.0 * (low_sq + EPS))
    high = 1.0 - inner / (2.0 * (high_sq + EPS))
    my_coef = jnp.where(core == 0, low, high)
    their_coef = jnp.where(core == 0, high, low)

    def comb_copy(n, step):
        q = across(step)
        return pltpu.make_async_remote_copy(
            src_ref=combs[n].at[q],
            dst_ref=recvs[n].at[chip],
            send_sem=comb_send.at[n, step],
            recv_sem=comb_recv.at[n, chip],
            device_id={"dp": q * 2 + core},
            device_id_type=MESH,
        )

    for n in range(ngroups):

        def send(step, carry, n=n):
            q = across(step)
            combs[n][q] = my_coef * grads[n][core, q] + their_coef * sibs[n][q]
            comb_copy(n, step).start()
            return carry

        lax.fori_loop(1, CHIPS, send, 0)
        recvs[n][chip] = my_coef * grads[n][core, chip] + their_coef * sibs[n][chip]

    for n in range(ngroups):

        def arrive(step, carry, n=n):
            q = across(step)
            pltpu.make_async_copy(recvs[n].at[q], recvs[n].at[q], comb_recv.at[n, q]).wait()
            return carry

        lax.fori_loop(1, CHIPS, arrive, 0)

        def against(s, carry, n=n):
            block = recvs[n][s]
            for t in range(CHIPS):
                part = fold(block * recvs[n][t])
                if n > 0:
                    part = part + pairs[s, t]
                pairs[s, t] = part
            return carry

        lax.fori_loop(0, CHIPS, against, 0)

    lane = lax.broadcasted_iota(jnp.int32, (CHIPS, LANES), 1)

    def collect(s, gram):
        column = jnp.sum(jnp.sum(pairs[s], axis=1), axis=1, keepdims=True)
        return gram + jnp.where(lane == s, column, 0.0)

    gram_src[...] = lax.fori_loop(0, CHIPS, collect, jnp.zeros((CHIPS, LANES), F32))

    gram_near[slot] = gram_src[...]

    def near_copy(step):
        c2, z2 = near(step)
        return pltpu.make_async_remote_copy(
            src_ref=gram_src,
            dst_ref=gram_near.at[slot],
            send_sem=near_send.at[step],
            recv_sem=near_recv.at[slot],
            device_id={"dp": chip * 2 + c2, "chan": z2},
            device_id_type=MESH,
        )

    def start_near(step, carry):
        near_copy(step).start()
        return carry

    def wait_near(step, carry):
        near_wait(step, gram_near, near_recv)
        return carry

    lax.fori_loop(1, 2 * DEPTH, start_near, 0)
    lax.fori_loop(1, 2 * DEPTH, wait_near, 0)
    gram_mid[...] = jnp.sum(gram_near[...], axis=0)
    gram_far[chip] = gram_mid[...]

    def far_copy(step):
        return pltpu.make_async_remote_copy(
            src_ref=gram_mid,
            dst_ref=gram_far.at[chip],
            send_sem=far_send.at[step],
            recv_sem=far_recv.at[chip],
            device_id={"dp": across(step) * 2 + core},
            device_id_type=MESH,
        )

    def start_far(step, carry):
        far_copy(step).start()
        return carry

    def wait_far(step, carry):
        q = across(step)
        pltpu.make_async_copy(gram_far.at[q], gram_far.at[q], far_recv.at[q]).wait()
        return carry

    lax.fori_loop(1, CHIPS, start_far, 0)
    lax.fori_loop(1, CHIPS, wait_far, 0)
    weights = pair_weights(jnp.sum(gram_far[...], axis=0))

    for (first, last), block in zip(GROUPS, recvs):
        for t in range(first, last):
            tap = weights[0:1] * block[0, t - first]
            for s in range(1, CHIPS):
                tap = tap + weights[s : s + 1] * block[s, t - first]
            out_ref[t] = tap

    for n in range(ngroups):
        swaps[n].wait_send()

    def near_left(step, carry):
        scal_copy(step).wait_send()
        near_copy(step).wait_send()
        return carry

    def far_left(step, carry):
        for n in range(ngroups):
            comb_copy(n, step).wait_send()
        far_copy(step).wait_send()
        return carry

    lax.fori_loop(1, 2 * DEPTH, near_left, 0)
    lax.fori_loop(1, CHIPS, far_left, 0)


def adasum(activations, out_grads):
    bf16 = jnp.bfloat16
    widths = [last - first for first, last in GROUPS]
    ngroups = len(GROUPS)
    scratch = [
        pltpu.VMEM((SAMPLES, SPACE, CIN), bf16),
        pltpu.VMEM((SAMPLES, SPACE, LANES), bf16),
        pltpu.VMEM((3, SPACE + 64, LANES), bf16),
    ]
    scratch += [pltpu.VMEM((2, CHIPS, w, ROWS, LANES), F32) for w in widths]
    scratch += [pltpu.VMEM((CHIPS, w, ROWS, LANES), F32) for _ in range(3) for w in widths]
    scratch += [
        pltpu.VMEM((3, 8, LANES), F32),
        pltpu.VMEM((2 * DEPTH, 3, 8, LANES), F32),
        pltpu.VMEM((CHIPS, CHIPS, 8, LANES), F32),
        pltpu.VMEM((CHIPS, LANES), F32),
        pltpu.VMEM((2 * DEPTH, CHIPS, LANES), F32),
        pltpu.VMEM((CHIPS, LANES), F32),
        pltpu.VMEM((CHIPS, CHIPS, LANES), F32),
    ]
    scratch += [
        pltpu.SemaphoreType.DMA(shape)
        for shape in (
            (SAMPLES,), (SAMPLES,), (ngroups,), (ngroups,), (2 * DEPTH,), (2 * DEPTH,),
            (ngroups, CHIPS), (ngroups, CHIPS), (2 * DEPTH,), (2 * DEPTH,), (CHIPS,), (CHIPS,),
        )
    ]
    return pl.pallas_call(
        kernel,
        out_shape=jax.ShapeDtypeStruct((9, ROWS, LANES), F32),
        in_specs=[pl.BlockSpec(memory_space=pl.ANY)] * 2,
        out_specs=pl.BlockSpec(memory_space=pltpu.VMEM),
        scratch_shapes=scratch,
        compiler_params=pltpu.CompilerParams(
            collective_id=0, has_side_effects=True, vmem_limit_bytes=62 << 20
        ),
        name="adasum",
    )(activations.reshape(SAMPLES, SPACE, CIN), out_grads.reshape(SAMPLES, SPACE, LANES))


def shards(activations, out_grads, weight, momentum):
    combined = adasum(activations, out_grads)
    combined = combined.transpose(1, 0, 2).reshape(weight.shape)
    new_momentum = 0.9 * momentum + combined
    new_weight = weight - 0.1 * new_momentum
    return new_weight, new_momentum


def solution(mesh):
    in_specs = (
        P("dp", None, None, None),
        P("dp", None, None, "chan"),
        P("dp", None, None, "chan"),
        P("dp", None, None, "chan"),
    )
    out_specs = (P("dp", None, None, "chan"), P("dp", None, None, "chan"))
    return jax.shard_map(shards, mesh=mesh, in_specs=in_specs, out_specs=out_specs, check_vma=False)
```

time: 432 us -> 58.6 us (0.14)
  blocking collectives: 321 us -> 0 us
  Pallas kernels: 0 us -> 56.2 us
  waiting for transfers between devices: 33.3 us -> 0 us
  other arithmetic: 26.6 us -> 1.56 us
  matrix products: 24.9 us -> 0 us
  between operations: 14.1 us -> 0.67 us
  local copies, waits for them, and re-layouts: 6.67 us -> 0.01 us
  starting transfers between devices: 4.66 us -> 0 us
    psum x5 -> x0, blocking collectives: 321 us -> none  [shards(): summed = lax.psum(slots, ('dp', 'chan'))]
    pallas_call x0 -> x1, Pallas kernels: none -> 56.2 us  [adasum(): pl.pallas_call(kernel, out_shape=jax.ShapeDtypeStruct((9, ROWS, LANES), F...]
    ppermute x5 -> x0, waiting for transfers between devices: 33.3 us -> none  [partner(): return lax.ppermute(block, axis, route)]
    dot_general x9 -> x0, matrix products: 24.9 us -> none  [local_gradient(): jnp.einsum('bhwc,bhwo->co', window, out_grads, preferred_element_type=jnp...]
    reduce_sum x9 -> x0, other arithmetic: 10.4 us -> none  [the longest x5 9.99 us: pair_partials(): jnp.sum(lower_vec * upper_vec)]
    another operation x4 -> x0, other arithmetic: 7.87 us -> none  [pair_partials(): jnp.stack([jnp.sum(lower_vec * upper_vec), jnp.sum(lower_vec * lower_vec)...]
    ppermute x5 -> x0, starting transfers between devices: 4.66 us -> none  [partner(): return lax.ppermute(block, axis, route)]
  transfers between devices with their start and end apart: 5 -> 0, of which waited for: 5 -> 0; matrix products, arithmetic and copies ran while one was open for 0% -> 0% of each run, Pallas kernels for 0% -> 0%
where the time goes in v1:
time: 58.6 us; the launch traced here: 58.5 us
  Pallas kernels  56.2 us (96%)
  other arithmetic  1.56 us (3%)
  between operations  0.67 us (1%)
    pallas_call x1, Pallas kernels, adasum(): pl.pallas_call(kernel, out_shape=jax.ShapeDtypeStruct((9, ROWS, LANES), F...  56.2 us
    sub x1, other arithmetic, shards(): new_weight = weight - 0.1 * new_momentum  1.56 us

profile of v1, /device:TPU:1, one launch (start us, length us, event | category | flops | bytes accessed | tf_op | source)
XLA Modules:
  0.0 58.5 jit_solution(8602213099860518102)
XLA Ops:
  0.6 0.0 copy-start.1
  0.6 0.0 copy-start
  0.7 56.2 %adasum.1 = f32[9,16,128]{2,1,0:T(8,128)} custom-call(bf16[8,1024,512]{2,1,0:T(8,128)(2,1)} %bitcast.5, bf16[8,1024,128]{2,1,0:T(8,128)(2,1)} %bitcast.6), custom_call_target="tpu_custom_call" | custom-call | tf_op jit(solution)/shard_map/adasum/pallas_call | solution.py:345
  56.9 0.0 copy-done.1
  56.9 0.0 copy-done
  56.9 1.6 %multiply_subtract_fusion = (f32[16,3,3,128]{3,0,2,1:T(8,128)}, f32[16,3,3,128]{3,0,2,1:T(8,128)}) fusion(f32[16,3,3,128]{3,0,2,1:T(8,128)S(1)} %copy-done, f32[16,3,3,128]{3,0,2,1:T(8,128)} %bitcast.7, f32[16,3,3,128]{3,0,2,1:T(8,128)S(1)} %copy-done.1), kind=kLoop, calls=%fused_computation | loop fusion | flops 73728 | bytes 368640 | tf_op jit(solution)/shard_map/sub | solution.py:362
Async XLA Ops:
  0.6 56.3 %copy-start.1 = (f32[16,3,3,128]{3,0,2,1:T(8,128)S(1)}, f32[16,3,3,128]{3,0,2,1:T(8,128)}, u32[]{:S(2)}) copy-start(f32[16,3,3,128]{3,0,2,1:T(8,128)} %param.7) | copy-start | bytes 221188
  0.6 56.3 %copy-start = (f32[16,3,3,128]{3,0,2,1:T(8,128)S(1)}, f32[16,3,3,128]{3,0,2,1:T(8,128)}, u32[]{:S(2)}) copy-start(f32[16,3,3,128]{3,0,2,1:T(8,128)} %param.6) | copy-start | bytes 221188

commit v2 on v0

v2 whole, which is shorter than its diff:
```python
import jax
import jax.numpy as jnp
from jax import lax
from jax.experimental import pallas as pl
from jax.experimental.pallas import tpu as pltpu
from jax.sharding import PartitionSpec as P

MESH = pl.DeviceIdType.MESH
SIDE = 4
CHIPS = SIDE * SIDE
DEPTH = 4
ROWS = 16
LANES = 128
SAMPLES = 8
SPACE = 1024
CIN = 512
TAPS = 9
EARLY = 4
MIDDLE = 7
F32 = jnp.float32
EPS = 1e-6


def fold(block):
    halves = block[:, :8] + block[:, 8:]
    return jnp.sum(halves, axis=0)


def total(part):
    return jnp.sum(jnp.sum(part, axis=0, keepdims=True), axis=1, keepdims=True)


def shifted(sample):
    wide = sample.astype(F32)
    column = lax.broadcasted_iota(jnp.int32, wide.shape, 0) % 32
    left = jnp.where(column == 31, 0.0, pltpu.roll(wide, SPACE - 1, 0))
    right = jnp.where(column == 0, 0.0, pltpu.roll(wide, 1, 0))
    return left.astype(sample.dtype), sample, right.astype(sample.dtype)


def pair_weights(gram):
    row = lax.broadcasted_iota(jnp.int32, gram.shape, 0)
    col = lax.broadcasted_iota(jnp.int32, gram.shape, 1)
    weights = jnp.ones((CHIPS, 1), F32)
    size = 1
    while size < CHIPS:
        mine = row // size == col // size
        other = jnp.logical_and(row // (2 * size) == col // (2 * size), jnp.logical_not(mine))
        mask = mine.astype(F32)
        own = gram * mask
        cross = gram * other.astype(F32)
        own_c = jnp.sum(own, axis=0, keepdims=True)
        cross_c = jnp.sum(cross, axis=0, keepdims=True)
        own_r = jnp.sum(own, axis=1, keepdims=True)
        cross_r = jnp.sum(cross, axis=1, keepdims=True)
        square_r = jnp.sum(mask * own_c, axis=1, keepdims=True)
        inner_r = jnp.sum(mask * cross_c, axis=1, keepdims=True)
        square_c = jnp.sum(mask * own_r, axis=0, keepdims=True)
        inner_c = jnp.sum(mask * cross_r, axis=0, keepdims=True)
        coef_r = 1.0 - inner_r / (2.0 * (jnp.maximum(square_r, 0.0) + EPS))
        coef_c = 1.0 - inner_c / (2.0 * (jnp.maximum(square_c, 0.0) + EPS))
        gram = gram * coef_r * coef_c
        weights = weights * coef_r
        size *= 2
    return weights


def kernel(act_hbm, og_hbm, out_ref, act, og, pad, grad_a, grad_b, grad_c, sib_a, sib_b, sib_c, raw, comb, block_a, block_b,
           scal_src, scal, coef_src, coef, pairs, gram_src, gram_near, gram_mid, gram_far,
           load_sem, og_sem, sib_send, sib_recv, raw_send, raw_recv, scal_send, scal_recv, coef_send, coef_recv,
           comb_send, comb_recv, near_send, near_recv, far_send, far_recv):
    dp = lax.axis_index("dp")
    z = lax.axis_index("chan")
    chip = dp // 2
    core = dp - chip * 2
    y = chip // SIDE
    x = chip - y * SIDE
    slot = core * DEPTH + z

    def wrap(value):
        return jnp.where(value >= SIDE, value - SIDE, value)

    rows_at = [y] + [wrap(y + d) * SIDE for d in range(SIDE)][1:]
    rows_at[0] = y * SIDE
    cols_at = [x] + [wrap(x + d) for d in range(1, SIDE)]
    chips = [rows_at[k // SIDE] + cols_at[k % SIDE] for k in range(1, CHIPS)]
    deep = [z] + [wrap(z + d) for d in range(1, DEPTH)]
    mates = [(core if k < DEPTH else 1 - core, deep[k % DEPTH]) for k in range(1, 2 * DEPTH)]

    for b in range(SAMPLES):
        pltpu.make_async_copy(og_hbm.at[b], og.at[b], og_sem.at[b]).start()
        pltpu.make_async_copy(act_hbm.at[b], act.at[b], load_sem.at[b]).start()

    barrier = pltpu.get_barrier_semaphore()
    for q in chips:
        pl.semaphore_signal(barrier, inc=1, device_id={"dp": q * 2 + core}, device_id_type=MESH)
        pl.semaphore_signal(barrier, inc=1, device_id={"dp": q * 2 + 1 - core}, device_id_type=MESH)
    for c2, z2 in mates:
        pl.semaphore_signal(barrier, inc=1, device_id={"dp": chip * 2 + c2, "chan": z2}, device_id_type=MESH)

    def remote(src, dst, send, recv, dp_to, z_to=None):
        to = {"dp": dp_to} if z_to is None else {"dp": dp_to, "chan": z_to}
        return pltpu.make_async_remote_copy(
            src_ref=src, dst_ref=dst, send_sem=send, recv_sem=recv, device_id=to, device_id_type=MESH
        )

    def landed(ref, sem):
        pltpu.make_async_copy(ref, ref, sem).wait()

    for j in range(3):
        for b in range(SAMPLES):
            pad[j, b, :32] = jnp.zeros((32, LANES), pad.dtype)
            pad[j, b, 32 + SPACE :] = jnp.zeros((32, LANES), pad.dtype)

    def columns(b, taps):
        return jnp.concatenate(
            [pad[t % 3, b, (2 - t // 3) * 32 : (2 - t // 3) * 32 + SPACE, :] for t in taps], axis=1
        )

    def store(grad, product, first):
        for t in range(product.shape[1] // LANES):
            tap = product[:, t * LANES : (t + 1) * LANES].reshape(CHIPS, 2, ROWS, LANES)
            for half in range(2):
                if first:
                    grad[half, :, t] = tap[:, half]
                else:
                    grad[half, :, t] += tap[:, half]

    def product(left, right):
        return lax.dot_general(left, right, (((0,), (0,)), ((), ())), preferred_element_type=F32)

    def move(b):
        for j, moved in enumerate(shifted(og[b])):
            pad[j, b, 32 : 32 + SPACE, :] = moved

    def early(b, carry, first=False, last=False):
        landed(act.at[b], load_sem.at[b])
        if not last:
            landed(og.at[b + 1], og_sem.at[b + 1])
        store(grad_a, product(act[b], columns(b, range(EARLY))), first)
        if not last:
            move(b + 1)
        return carry

    def later(grad, taps, span):
        def body(k, carry, first=False):
            left = act[pl.ds(span * k, span)].reshape(span * SPACE, CIN)
            right = jnp.concatenate([columns(span * k + n, taps) for n in range(span)], axis=0)
            store(grad, product(left, right), first)
            return carry

        body(0, 0, True)
        lax.fori_loop(1, SAMPLES // span, body, 0)

    landed(og.at[0], og_sem.at[0])
    move(0)
    early(0, 0, first=True)
    lax.fori_loop(1, SAMPLES - 1, early, 0)
    early(SAMPLES - 1, 0, last=True)

    pl.semaphore_wait(barrier, 2 * (CHIPS - 1) + 2 * DEPTH - 1)

    def swap(n, grad, sib):
        copy = remote(grad.at[1 - core], sib, sib_send.at[n], sib_recv.at[n], chip * 2 + 1 - core)
        copy.start()
        return copy

    swaps = [swap(0, grad_a, sib_a)]
    for q in chips:
        for half in range(2):
            remote(
                grad_a.at[half, q], raw.at[core, chip], raw_send.at[half], raw_recv.at[core], q * 2 + half
            ).start()

    later(grad_b, range(EARLY, MIDDLE), 2)
    swaps.append(swap(1, grad_b, sib_b))
    later(grad_c, range(MIDDLE, TAPS), 4)
    swaps.append(swap(2, grad_c, sib_c))

    def products(grad, sib, sums):
        def body(q, carry):
            mine = grad[core, q]
            theirs = sib[q]
            return (
                carry[0] + fold(mine * theirs),
                carry[1] + fold(mine * mine),
                carry[2] + fold(theirs * theirs),
            )

        return lax.fori_loop(0, CHIPS, body, sums)

    zero = jnp.zeros((8, LANES), F32)
    sums = (zero, zero, zero)
    for copy, grad, sib in zip(swaps, (grad_a, grad_b, grad_c), (sib_a, sib_b, sib_c)):
        copy.wait_recv()
        sums = products(grad, sib, sums)
    scal_src[0] = sums[0]
    scal_src[1] = jnp.where(core == 0, sums[1], sums[2])
    scal_src[2] = jnp.where(core == 0, sums[2], sums[1])
    for c2, z2 in mates:
        remote(scal_src, scal.at[slot], scal_send.at[0], scal_recv.at[0], chip * 2 + c2, z2).start()
    scal[slot] = scal_src[...]
    landed(scal.at[: 2 * DEPTH - 1], scal_recv.at[0])
    added = jnp.sum(scal[...], axis=0)
    inner, low_sq, high_sq = total(added[0]), total(added[1]), total(added[2])
    low = 1.0 - inner / (2.0 * (low_sq + EPS))
    high = 1.0 - inner / (2.0 * (high_sq + EPS))
    coef_src[0:1] = jnp.broadcast_to(low, (1, LANES))
    coef_src[1:2] = jnp.broadcast_to(high, (1, LANES))
    my_coef = jnp.where(core == 0, low, high)
    their_coef = jnp.where(core == 0, high, low)

    wide = MIDDLE - EARLY
    for k, q in enumerate(chips):
        remote(coef_src, coef.at[chip], coef_send.at[0], coef_recv.at[0], q * 2 + core).start()
        comb[k, :wide] = my_coef * grad_b[core, q] + their_coef * sib_b[q]
        comb[k, wide:] = my_coef * grad_c[core, q] + their_coef * sib_c[q]
        remote(comb.at[k], block_b.at[chip], comb_send.at[0], comb_recv.at[0], q * 2 + core).start()
    block_b[chip, :wide] = my_coef * grad_b[core, chip] + their_coef * sib_b[chip]
    block_b[chip, wide:] = my_coef * grad_c[core, chip] + their_coef * sib_c[chip]
    block_a[chip] = my_coef * grad_a[core, chip] + their_coef * sib_a[chip]
    for half in range(2):
        landed(raw.at[half, : CHIPS - 1], raw_recv.at[half])
    landed(coef.at[: CHIPS - 1], coef_recv.at[0])
    for q in chips:
        block_a[q] = coef[q, 0:1] * raw[0, q] + coef[q, 1:2] * raw[1, q]

    def against(block, more):
        def body(s, carry):
            mine = block[s]
            for t in range(CHIPS):
                part = fold(mine * block[t])
                pairs[s, t] = part + pairs[s, t] if more else part
            return carry

        lax.fori_loop(0, CHIPS, body, 0)

    against(block_a, False)
    landed(block_b.at[: CHIPS - 1], comb_recv.at[0])
    against(block_b, True)

    sums = jnp.sum(jnp.sum(pairs[...].reshape(CHIPS * CHIPS, 8, LANES), axis=1), axis=1, keepdims=True)
    index = lax.broadcasted_iota(jnp.int32, (CHIPS * CHIPS, LANES), 0)
    lane = lax.broadcasted_iota(jnp.int32, (CHIPS * CHIPS, LANES), 1)
    spread = jnp.where(lane == index // CHIPS, sums, 0.0)
    gram_src[...] = jnp.sum(spread.reshape(CHIPS, CHIPS, LANES), axis=0)

    for c2, z2 in mates:
        remote(gram_src, gram_near.at[slot], near_send.at[0], near_recv.at[0], chip * 2 + c2, z2).start()
    gram_near[slot] = gram_src[...]
    for copy in swaps:
        copy.wait_send()
    for half in range(2):
        landed(raw.at[half, : CHIPS - 1], raw_send.at[half])
    landed(scal.at[: 2 * DEPTH - 1], scal_send.at[0])
    landed(coef.at[: CHIPS - 1], coef_send.at[0])
    landed(comb, comb_send.at[0])
    landed(gram_near.at[: 2 * DEPTH - 1], near_recv.at[0])
    gram_mid[...] = jnp.sum(gram_near[...], axis=0)
    for q in chips:
        remote(gram_mid, gram_far.at[chip], far_send.at[0], far_recv.at[0], q * 2 + core).start()
    gram_far[chip] = gram_mid[...]
    landed(gram_near.at[: 2 * DEPTH - 1], near_send.at[0])
    landed(gram_far.at[: CHIPS - 1], far_recv.at[0])
    weights = pair_weights(jnp.sum(gram_far[...], axis=0))

    for t in range(TAPS):
        block, u = (block_a, t) if t < EARLY else (block_b, t - EARLY)
        tap = weights[0:1] * block[0, u]
        for s in range(1, CHIPS):
            tap = tap + weights[s : s + 1] * block[s, u]
        out_ref[t] = tap
    landed(gram_far.at[: CHIPS - 1], far_send.at[0])


def adasum(activations, out_grads):
    bf16 = jnp.bfloat16
    late = TAPS - EARLY
    scratch = [
        pltpu.VMEM((SAMPLES, SPACE, CIN), bf16),
        pltpu.VMEM((SAMPLES, SPACE, LANES), bf16),
        pltpu.VMEM((3, SAMPLES, SPACE + 64, LANES), bf16),
    ]
    scratch += [
        pltpu.VMEM(shape, F32)
        for shape in (
            (2, CHIPS, EARLY, ROWS, LANES),
            (2, CHIPS, MIDDLE - EARLY, ROWS, LANES),
            (2, CHIPS, TAPS - MIDDLE, ROWS, LANES),
            (CHIPS, EARLY, ROWS, LANES),
            (CHIPS, MIDDLE - EARLY, ROWS, LANES),
            (CHIPS, TAPS - MIDDLE, ROWS, LANES),
            (2, CHIPS, EARLY, ROWS, LANES),
            (CHIPS - 1, late, ROWS, LANES),
            (CHIPS, EARLY, ROWS, LANES),
            (CHIPS, late, ROWS, LANES),
            (3, 8, LANES),
            (2 * DEPTH, 3, 8, LANES),
            (2, LANES),
            (CHIPS, 2, LANES),
            (CHIPS, CHIPS, 8, LANES),
            (CHIPS, LANES),
            (2 * DEPTH, CHIPS, LANES),
            (CHIPS, LANES),
            (CHIPS, CHIPS, LANES),
        )
    ]
    scratch += [
        pltpu.SemaphoreType.DMA(shape)
        for shape in (
            (SAMPLES,), (SAMPLES,), (3,), (3,), (2,), (2,), (1,), (1,), (1,), (1,), (1,), (1,), (1,), (1,), (1,), (1,),
        )
    ]
    return pl.pallas_call(
        kernel,
        out_shape=jax.ShapeDtypeStruct((9, ROWS, LANES), F32),
        in_specs=[pl.BlockSpec(memory_space=pltpu.HBM)] * 2,
        out_specs=pl.BlockSpec(memory_space=pltpu.VMEM),
        scratch_shapes=scratch,
        compiler_params=pltpu.CompilerParams(
            collective_id=0, has_side_effects=True, vmem_limit_bytes=52 << 20
        ),
        name="adasum",
    )(activations.reshape(SAMPLES, SPACE, CIN), out_grads.reshape(SAMPLES, SPACE, LANES))


def shards(activations, out_grads, weight, momentum):
    combined = adasum(activations, out_grads)
    combined = combined.transpose(1, 0, 2).reshape(weight.shape)
    new_momentum = 0.9 * momentum + combined
    new_weight = weight - 0.1 * new_momentum
    return new_weight, new_momentum


def solution(mesh):
    in_specs = (
        P("dp", None, None, None),
        P("dp", None, None, "chan"),
        P("dp", None, None, "chan"),
        P("dp", None, None, "chan"),
    )
    out_specs = (P("dp", None, None, "chan"), P("dp", None, None, "chan"))
    return jax.shard_map(shards, mesh=mesh, in_specs=in_specs, out_specs=out_specs, check_vma=False)
```

time: 432 us -> 50 us (0.12)
  blocking collectives: 321 us -> 0 us
  Pallas kernels: 0 us -> 48.6 us
  waiting for transfers between devices: 33.3 us -> 0 us
  other arithmetic: 26.6 us -> 0.68 us
  matrix products: 24.9 us -> 0 us
  between operations: 14.1 us -> 0.67 us
  local copies, waits for them, and re-layouts: 6.67 us -> 0.01 us
  starting transfers between devices: 4.66 us -> 0 us
    psum x5 -> x0, blocking collectives: 321 us -> none  [shards(): summed = lax.psum(slots, ('dp', 'chan'))]
    pallas_call x0 -> x1, Pallas kernels: none -> 48.6 us  [adasum(): pl.pallas_call(kernel, out_shape=jax.ShapeDtypeStruct((9, ROWS, LANES), F...]
    ppermute x5 -> x0, waiting for transfers between devices: 33.3 us -> none  [partner(): return lax.ppermute(block, axis, route)]
    dot_general x9 -> x0, matrix products: 24.9 us -> none  [local_gradient(): jnp.einsum('bhwc,bhwo->co', window, out_grads, preferred_element_type=jnp...]
    reduce_sum x9 -> x0, other arithmetic: 10.4 us -> none  [the longest x5 9.99 us: pair_partials(): jnp.sum(lower_vec * upper_vec)]
    another operation x4 -> x0, other arithmetic: 7.87 us -> none  [pair_partials(): jnp.stack([jnp.sum(lower_vec * upper_vec), jnp.sum(lower_vec * lower_vec)...]
    ppermute x5 -> x0, starting transfers between devices: 4.66 us -> none  [partner(): return lax.ppermute(block, axis, route)]
  transfers between devices with their start and end apart: 5 -> 0, of which waited for: 5 -> 0; matrix products, arithmetic and copies ran while one was open for 0% -> 0% of each run, Pallas kernels for 0% -> 0%
where the time goes in v2:
time: 50 us; the launch traced here: 49.9 us
  Pallas kernels  48.6 us (97%)
  other arithmetic  0.68 us (1%)
  between operations  0.67 us (1%)
    pallas_call x1, Pallas kernels, adasum(): pl.pallas_call(kernel, out_shape=jax.ShapeDtypeStruct((9, ROWS, LANES), F...  48.6 us

profile of v2, /device:TPU:1, one launch (start us, length us, event | category | flops | bytes accessed | tf_op | source)
XLA Modules:
  0.0 49.9 jit_solution(17315244544527319885)
XLA Ops:
  0.6 0.0 copy-start.1
  0.6 0.0 copy-start
  0.7 48.6 %adasum.1 = f32[9,16,128]{2,1,0:T(8,128)S(1)} custom-call(bf16[8,1024,512]{2,1,0:T(8,128)(2,1)} %bitcast.6, bf16[8,1024,128]{2,1,0:T(8,128)(2,1)} %bitcast.7), custom_call_target="tpu_custom_call" | custom-call | tf_op jit(solution)/shard_map/adasum/pallas_call | solution.py:314
  49.2 0.0 copy-done.1
  49.2 0.0 copy-done
  49.3 0.7 %multiply_subtract_fusion = (f32[16,3,3,128]{3,0,2,1:T(8,128)}, f32[16,3,3,128]{3,0,2,1:T(8,128)}) fusion(f32[16,3,3,128]{3,0,2,1:T(8,128)S(1)} %copy-done, f32[16,3,3,128]{3,0,2,1:T(8,128)S(1)} %bitcast.5, f32[16,3,3,128]{3,0,2,1:T(8,128)S(1)} %copy-done.1), kind=kLoop, calls=%fused_computation | loop fusion | flops 73728 | bytes 368640 | tf_op jit(solution)/shard_map/sub | solution.py:331
Async XLA Ops:
  0.6 48.6 %copy-start.1 = (f32[16,3,3,128]{3,0,2,1:T(8,128)S(1)}, f32[16,3,3,128]{3,0,2,1:T(8,128)}, u32[]{:S(2)}) copy-start(f32[16,3,3,128]{3,0,2,1:T(8,128)} %param.7) | copy-start | bytes 221188
  0.6 48.6 %copy-start = (f32[16,3,3,128]{3,0,2,1:T(8,128)S(1)}, f32[16,3,3,128]{3,0,2,1:T(8,128)}, u32[]{:S(2)}) copy-start(f32[16,3,3,128]{3,0,2,1:T(8,128)} %param.6) | copy-start | bytes 221188

commit v3 on v2

--- a/solution.py
+++ b/solution.py
@@ -19,6 +19,21 @@
 MIDDLE = 7
 F32 = jnp.float32
 EPS = 1e-6
+ROUTE = (
+    (2, 2), (0, 1), (2, 1), (1, 0), (1, 2), (0, 3), (2, 3), (3, 0), (3, 2), (1, 1), (2, 0), (3, 3), (0, 2), (1, 3), (3, 1),
+)
+PACKED = 8
+
+
+def hops(step):
+    return sum(min(d, SIDE - d) for d in (step[0], step[1], step[3]))
+
+
+EVERYONE = sorted(
+    [(dy, dx, dc, dz) for dy in range(SIDE) for dx in range(SIDE) for dc in range(2) for dz in range(DEPTH)][1:],
+    key=lambda step: -hops(step),
+)
+DEVICES = len(EVERYONE) + 1
 
 
 def fold(block):
@@ -66,9 +81,9 @@
 
 
 def kernel(act_hbm, og_hbm, out_ref, act, og, pad, grad_a, grad_b, grad_c, sib_a, sib_b, sib_c, raw, comb, block_a, block_b,
-           scal_src, scal, coef_src, coef, pairs, gram_src, gram_near, gram_mid, gram_far,
+           scal_src, scal, coef_src, coef, pairs, gram_src, gram_all,
            load_sem, og_sem, sib_send, sib_recv, raw_send, raw_recv, scal_send, scal_recv, coef_send, coef_recv,
-           comb_send, comb_recv, near_send, near_recv, far_send, far_recv):
+           comb_send, comb_recv, gram_send, gram_recv):
     dp = lax.axis_index("dp")
     z = lax.axis_index("chan")
     chip = dp // 2
@@ -83,7 +98,7 @@
     rows_at = [y] + [wrap(y + d) * SIDE for d in range(SIDE)][1:]
     rows_at[0] = y * SIDE
     cols_at = [x] + [wrap(x + d) for d in range(1, SIDE)]
-    chips = [rows_at[k // SIDE] + cols_at[k % SIDE] for k in range(1, CHIPS)]
+    chips = [rows_at[dy] + cols_at[dx] for dy, dx in ROUTE]
     deep = [z] + [wrap(z + d) for d in range(1, DEPTH)]
     mates = [(core if k < DEPTH else 1 - core, deep[k % DEPTH]) for k in range(1, 2 * DEPTH)]
 
@@ -92,11 +107,11 @@
         pltpu.make_async_copy(act_hbm.at[b], act.at[b], load_sem.at[b]).start()
 
     barrier = pltpu.get_barrier_semaphore()
-    for q in chips:
-        pl.semaphore_signal(barrier, inc=1, device_id={"dp": q * 2 + core}, device_id_type=MESH)
-        pl.semaphore_signal(barrier, inc=1, device_id={"dp": q * 2 + 1 - core}, device_id_type=MESH)
-    for c2, z2 in mates:
-        pl.semaphore_signal(barrier, inc=1, device_id={"dp": chip * 2 + c2, "chan": z2}, device_id_type=MESH)
+    everyone = [
+        (rows_at[dy] * 2 + cols_at[dx] * 2 + (1 - core if dc else core), deep[dz]) for dy, dx, dc, dz in EVERYONE
+    ]
+    for device, level in everyone:
+        pl.semaphore_signal(barrier, inc=1, device_id={"dp": device, "chan": level}, device_id_type=MESH)
 
     def remote(src, dst, send, recv, dp_to, z_to=None):
         to = {"dp": dp_to} if z_to is None else {"dp": dp_to, "chan": z_to}
@@ -158,7 +173,7 @@
     lax.fori_loop(1, SAMPLES - 1, early, 0)
     early(SAMPLES - 1, 0, last=True)
 
-    pl.semaphore_wait(barrier, 2 * (CHIPS - 1) + 2 * DEPTH - 1)
+    pl.semaphore_wait(barrier, DEVICES - 1)
 
     def swap(n, grad, sib):
         copy = remote(grad.at[1 - core], sib, sib_send.at[n], sib_recv.at[n], chip * 2 + 1 - core)
@@ -242,12 +257,13 @@
     sums = jnp.sum(jnp.sum(pairs[...].reshape(CHIPS * CHIPS, 8, LANES), axis=1), axis=1, keepdims=True)
     index = lax.broadcasted_iota(jnp.int32, (CHIPS * CHIPS, LANES), 0)
     lane = lax.broadcasted_iota(jnp.int32, (CHIPS * CHIPS, LANES), 1)
-    spread = jnp.where(lane == index // CHIPS, sums, 0.0)
-    gram_src[...] = jnp.sum(spread.reshape(CHIPS, CHIPS, LANES), axis=0)
-
-    for c2, z2 in mates:
-        remote(gram_src, gram_near.at[slot], near_send.at[0], near_recv.at[0], chip * 2 + c2, z2).start()
-    gram_near[slot] = gram_src[...]
+    spread = jnp.where(lane == index % (CHIPS * PACKED), sums, 0.0)
+    gram_src[...] = jnp.sum(spread.reshape(2, CHIPS * PACKED, LANES), axis=1)
+
+    here = dp * DEPTH + z
+    for device, level in everyone:
+        remote(gram_src, gram_all.at[here], gram_send.at[0], gram_recv.at[0], device, level).start()
+    gram_all[here] = gram_src[...]
     for copy in swaps:
         copy.wait_send()
     for half in range(2):
@@ -255,14 +271,15 @@
     landed(scal.at[: 2 * DEPTH - 1], scal_send.at[0])
     landed(coef.at[: CHIPS - 1], coef_send.at[0])
     landed(comb, comb_send.at[0])
-    landed(gram_near.at[: 2 * DEPTH - 1], near_recv.at[0])
-    gram_mid[...] = jnp.sum(gram_near[...], axis=0)
-    for q in chips:
-        remote(gram_mid, gram_far.at[chip], far_send.at[0], far_recv.at[0], q * 2 + core).start()
-    gram_far[chip] = gram_mid[...]
-    landed(gram_near.at[: 2 * DEPTH - 1], near_send.at[0])
-    landed(gram_far.at[: CHIPS - 1], far_recv.at[0])
-    weights = pair_weights(jnp.sum(gram_far[...], axis=0))
+    landed(gram_all.at[: DEVICES - 1], gram_recv.at[0])
+    packed = jnp.sum(gram_all[...], axis=0)
+    rows = jnp.concatenate([jnp.broadcast_to(packed[n : n + 1], (PACKED, LANES)) for n in range(2)], axis=0)
+    row = lax.broadcasted_iota(jnp.int32, (CHIPS, LANES), 0) % PACKED
+    gram = rows
+    for n in range(1, PACKED):
+        gram = jnp.where(row == n, pltpu.roll(rows, LANES - CHIPS * n, 1), gram)
+    gram = jnp.where(lax.broadcasted_iota(jnp.int32, (CHIPS, LANES), 1) < CHIPS, gram, 0.0)
+    weights = pair_weights(gram)
 
     for t in range(TAPS):
         block, u = (block_a, t) if t < EARLY else (block_b, t - EARLY)
@@ -270,7 +287,7 @@
         for s in range(1, CHIPS):
             tap = tap + weights[s : s + 1] * block[s, u]
         out_ref[t] = tap
-    landed(gram_far.at[: CHIPS - 1], far_send.at[0])
+    landed(gram_all.at[: DEVICES - 1], gram_send.at[0])
 
 
 def adasum(activations, out_grads):
@@ -299,16 +316,14 @@
             (2, LANES),
             (CHIPS, 2, LANES),
             (CHIPS, CHIPS, 8, LANES),
-            (CHIPS, LANES),
-            (2 * DEPTH, CHIPS, LANES),
-            (CHIPS, LANES),
-            (CHIPS, CHIPS, LANES),
+            (2, LANES),
+            (DEVICES, 2, LANES),
         )
     ]
     scratch += [
         pltpu.SemaphoreType.DMA(shape)
         for shape in (
-            (SAMPLES,), (SAMPLES,), (3,), (3,), (2,), (2,), (1,), (1,), (1,), (1,), (1,), (1,), (1,), (1,), (1,), (1,),
+            (SAMPLES,), (SAMPLES,), (3,), (3,), (2,), (2,), (1,), (1,), (1,), (1,), (1,), (1,), (1,), (1,),
         )
     ]
     return pl.pallas_call(

time: 50 us -> 46.7 us (0.934)
  Pallas kernels: 48.6 us -> 45.2 us
    pallas_call x1, Pallas kernels: 48.6 us -> 45.2 us  [adasum(): pl.pallas_call(kernel, out_shape=jax.ShapeDtypeStruct((9, ROWS, LANES), F...]
where the time goes in v3:
time: 46.7 us; the launch traced here: 46.6 us
  Pallas kernels  45.2 us (97%)
  other arithmetic  0.68 us (1%)
  between operations  0.67 us (1%)
    pallas_call x1, Pallas kernels, adasum(): pl.pallas_call(kernel, out_shape=jax.ShapeDtypeStruct((9, ROWS, LANES), F...  45.2 us

profile of v3, /device:TPU:1, one launch (start us, length us, event | category | flops | bytes accessed | tf_op | source)
XLA Modules:
  0.0 46.6 jit_solution(14285658897691004738)
XLA Ops:
  0.6 0.0 copy-start.1
  0.6 0.0 copy-start
  0.7 45.2 %adasum.1 = f32[9,16,128]{2,1,0:T(8,128)S(1)} custom-call(bf16[8,1024,512]{2,1,0:T(8,128)(2,1)} %bitcast.6, bf16[8,1024,128]{2,1,0:T(8,128)(2,1)} %bitcast.7), custom_call_target="tpu_custom_call" | custom-call | tf_op jit(solution)/shard_map/adasum/pallas_call | solution.py:329
  45.9 0.0 copy-done.1
  45.9 0.0 copy-done
  45.9 0.7 %multiply_subtract_fusion = (f32[16,3,3,128]{3,0,2,1:T(8,128)}, f32[16,3,3,128]{3,0,2,1:T(8,128)}) fusion(f32[16,3,3,128]{3,0,2,1:T(8,128)S(1)} %copy-done, f32[16,3,3,128]{3,0,2,1:T(8,128)S(1)} %bitcast.5, f32[16,3,3,128]{3,0,2,1:T(8,128)S(1)} %copy-done.1), kind=kLoop, calls=%fused_computation | loop fusion | flops 73728 | bytes 368640 | tf_op jit(solution)/shard_map/sub | solution.py:346
Async XLA Ops:
  0.6 45.2 %copy-start.1 = (f32[16,3,3,128]{3,0,2,1:T(8,128)S(1)}, f32[16,3,3,128]{3,0,2,1:T(8,128)}, u32[]{:S(2)}) copy-start(f32[16,3,3,128]{3,0,2,1:T(8,128)} %param.7) | copy-start | bytes 221188
  0.6 45.2 %copy-start = (f32[16,3,3,128]{3,0,2,1:T(8,128)S(1)}, f32[16,3,3,128]{3,0,2,1:T(8,128)}, u32[]{:S(2)}) copy-start(f32[16,3,3,128]{3,0,2,1:T(8,128)} %param.6) | copy-start | bytes 221188

commit v4 on v3

--- a/solution.py
+++ b/solution.py
@@ -16,7 +16,8 @@
 CIN = 512
 TAPS = 9
 EARLY = 4
-MIDDLE = 7
+MIDDLE = 8
+RAW = 5
 F32 = jnp.float32
 EPS = 1e-6
 ROUTE = (
@@ -80,7 +81,7 @@
     return weights
 
 
-def kernel(act_hbm, og_hbm, out_ref, act, og, pad, grad_a, grad_b, grad_c, sib_a, sib_b, sib_c, raw, comb, block_a, block_b,
+def kernel(act_hbm, og_hbm, out_ref, act, og, pad, grad_a, grad_b, grad_c, sib_a, sib_b, sib_c, raw_a, raw_b, comb_b, comb_c, block_a, block_b, block_c,
            scal_src, scal, coef_src, coef, pairs, gram_src, gram_all,
            load_sem, og_sem, sib_send, sib_recv, raw_send, raw_recv, scal_send, scal_recv, coef_send, coef_recv,
            comb_send, comb_recv, gram_send, gram_recv):
@@ -110,8 +111,11 @@
     everyone = [
         (rows_at[dy] * 2 + cols_at[dx] * 2 + (1 - core if dc else core), deep[dz]) for dy, dx, dc, dz in EVERYONE
     ]
-    for device, level in everyone:
-        pl.semaphore_signal(barrier, inc=1, device_id={"dp": device, "chan": level}, device_id_type=MESH)
+    for q in chips:
+        for half in range(2):
+            pl.semaphore_signal(barrier, inc=1, device_id={"dp": q * 2 + half}, device_id_type=MESH)
+    for c2, z2 in mates:
+        pl.semaphore_signal(barrier, inc=1, device_id={"dp": chip * 2 + c2, "chan": z2}, device_id_type=MESH)
 
     def remote(src, dst, send, recv, dp_to, z_to=None):
         to = {"dp": dp_to} if z_to is None else {"dp": dp_to, "chan": z_to}
@@ -173,7 +177,7 @@
     lax.fori_loop(1, SAMPLES - 1, early, 0)
     early(SAMPLES - 1, 0, last=True)
 
-    pl.semaphore_wait(barrier, DEVICES - 1)
+    pl.semaphore_wait(barrier, 2 * (CHIPS - 1) + 2 * DEPTH - 1)
 
     def swap(n, grad, sib):
         copy = remote(grad.at[1 - core], sib, sib_send.at[n], sib_recv.at[n], chip * 2 + 1 - core)
@@ -184,11 +188,20 @@
     for q in chips:
         for half in range(2):
             remote(
-                grad_a.at[half, q], raw.at[core, chip], raw_send.at[half], raw_recv.at[core], q * 2 + half
+                grad_a.at[half, q], raw_a.at[core, chip], raw_send.at[half], raw_recv.at[core], q * 2 + half
             ).start()
 
     later(grad_b, range(EARLY, MIDDLE), 2)
     swaps.append(swap(1, grad_b, sib_b))
+    for q in chips:
+        for half in range(2):
+            remote(
+                grad_b.at[half, q, : RAW - EARLY],
+                raw_b.at[core, chip],
+                raw_send.at[2 + half],
+                raw_recv.at[2 + core],
+                q * 2 + half,
+            ).start()
     later(grad_c, range(MIDDLE, TAPS), 4)
     swaps.append(swap(2, grad_c, sib_c))
 
@@ -202,7 +215,7 @@
                 carry[2] + fold(theirs * theirs),
             )
 
-        return lax.fori_loop(0, CHIPS, body, sums)
+        return lax.fori_loop(0, CHIPS, body, sums, unroll=4)
 
     zero = jnp.zeros((8, LANES), F32)
     sums = (zero, zero, zero)
@@ -225,20 +238,29 @@
     my_coef = jnp.where(core == 0, low, high)
     their_coef = jnp.where(core == 0, high, low)
 
-    wide = MIDDLE - EARLY
+    skip = RAW - EARLY
+
+    def mixed(mine, theirs):
+        return my_coef * mine + their_coef * theirs
+
     for k, q in enumerate(chips):
         remote(coef_src, coef.at[chip], coef_send.at[0], coef_recv.at[0], q * 2 + core).start()
-        comb[k, :wide] = my_coef * grad_b[core, q] + their_coef * sib_b[q]
-        comb[k, wide:] = my_coef * grad_c[core, q] + their_coef * sib_c[q]
-        remote(comb.at[k], block_b.at[chip], comb_send.at[0], comb_recv.at[0], q * 2 + core).start()
-    block_b[chip, :wide] = my_coef * grad_b[core, chip] + their_coef * sib_b[chip]
-    block_b[chip, wide:] = my_coef * grad_c[core, chip] + their_coef * sib_c[chip]
-    block_a[chip] = my_coef * grad_a[core, chip] + their_coef * sib_a[chip]
+        comb_b[k] = mixed(grad_b[core, q, skip:], sib_b[q, skip:])
+        remote(comb_b.at[k], block_b.at[chip], comb_send.at[0], comb_recv.at[0], q * 2 + core).start()
+    for k, q in enumerate(chips):
+        comb_c[k] = mixed(grad_c[core, q], sib_c[q])
+        remote(comb_c.at[k], block_c.at[chip], comb_send.at[1], comb_recv.at[1], q * 2 + core).start()
+    block_b[chip] = mixed(grad_b[core, chip, skip:], sib_b[chip, skip:])
+    block_c[chip] = mixed(grad_c[core, chip], sib_c[chip])
+    block_a[chip, :EARLY] = my_coef * grad_a[core, chip] + their_coef * sib_a[chip]
+    block_a[chip, EARLY:] = my_coef * grad_b[core, chip, :skip] + their_coef * sib_b[chip, :skip]
     for half in range(2):
-        landed(raw.at[half, : CHIPS - 1], raw_recv.at[half])
+        landed(raw_a.at[half, : CHIPS - 1], raw_recv.at[half])
+        landed(raw_b.at[half, : CHIPS - 1], raw_recv.at[2 + half])
     landed(coef.at[: CHIPS - 1], coef_recv.at[0])
     for q in chips:
-        block_a[q] = coef[q, 0:1] * raw[0, q] + coef[q, 1:2] * raw[1, q]
+        block_a[q, :EARLY] = coef[q, 0:1] * raw_a[0, q] + coef[q, 1:2] * raw_a[1, q]
+        block_a[q, EARLY:] = coef[q, 0:1] * raw_b[0, q] + coef[q, 1:2] * raw_b[1, q]
 
     def against(block, more):
         def body(s, carry):
@@ -253,6 +275,8 @@
     against(block_a, False)
     landed(block_b.at[: CHIPS - 1], comb_recv.at[0])
     against(block_b, True)
+    landed(block_c.at[: CHIPS - 1], comb_recv.at[1])
+    against(block_c, True)
 
     sums = jnp.sum(jnp.sum(pairs[...].reshape(CHIPS * CHIPS, 8, LANES), axis=1), axis=1, keepdims=True)
     index = lax.broadcasted_iota(jnp.int32, (CHIPS * CHIPS, LANES), 0)
@@ -267,10 +291,12 @@
     for copy in swaps:
         copy.wait_send()
     for half in range(2):
-        landed(raw.at[half, : CHIPS - 1], raw_send.at[half])
+        landed(raw_a.at[half, : CHIPS - 1], raw_send.at[half])
+        landed(raw_b.at[half, : CHIPS - 1], raw_send.at[2 + half])
     landed(scal.at[: 2 * DEPTH - 1], scal_send.at[0])
     landed(coef.at[: CHIPS - 1], coef_send.at[0])
-    landed(comb, comb_send.at[0])
+    landed(comb_b, comb_send.at[0])
+    landed(comb_c, comb_send.at[1])
     landed(gram_all.at[: DEVICES - 1], gram_recv.at[0])
     packed = jnp.sum(gram_all[...], axis=0)
     rows = jnp.concatenate([jnp.broadcast_to(packed[n : n + 1], (PACKED, LANES)) for n in range(2)], axis=0)
@@ -282,7 +308,7 @@
     weights = pair_weights(gram)
 
     for t in range(TAPS):
-        block, u = (block_a, t) if t < EARLY else (block_b, t - EARLY)
+        block, u = (block_a, t) if t < RAW else (block_b, t - RAW) if t < MIDDLE else (block_c, t - MIDDLE)
         tap = weights[0:1] * block[0, u]
         for s in range(1, CHIPS):
             tap = tap + weights[s : s + 1] * block[s, u]
@@ -292,7 +318,6 @@
 
 def adasum(activations, out_grads):
     bf16 = jnp.bfloat16
-    late = TAPS - EARLY
     scratch = [
         pltpu.VMEM((SAMPLES, SPACE, CIN), bf16),
         pltpu.VMEM((SAMPLES, SPACE, LANES), bf16),
@@ -308,9 +333,12 @@
             (CHIPS, MIDDLE - EARLY, ROWS, LANES),
             (CHIPS, TAPS - MIDDLE, ROWS, LANES),
             (2, CHIPS, EARLY, ROWS, LANES),
-            (CHIPS - 1, late, ROWS, LANES),
-            (CHIPS, EARLY, ROWS, LANES),
-            (CHIPS, late, ROWS, LANES),
+            (2, CHIPS, RAW - EARLY, ROWS, LANES),
+            (CHIPS - 1, MIDDLE - RAW, ROWS, LANES),
+            (CHIPS - 1, TAPS - MIDDLE, ROWS, LANES),
+            (CHIPS, RAW, ROWS, LANES),
+            (CHIPS, MIDDLE - RAW, ROWS, LANES),
+            (CHIPS, TAPS - MIDDLE, ROWS, LANES),
             (3, 8, LANES),
             (2 * DEPTH, 3, 8, LANES),
             (2, LANES),
@@ -323,7 +351,7 @@
     scratch += [
         pltpu.SemaphoreType.DMA(shape)
         for shape in (
-            (SAMPLES,), (SAMPLES,), (3,), (3,), (2,), (2,), (1,), (1,), (1,), (1,), (1,), (1,), (1,), (1,),
+            (SAMPLES,), (SAMPLES,), (3,), (3,), (4,), (4,), (1,), (1,), (1,), (1,), (2,), (2,), (1,), (1,),
         )
     ]
     return pl.pallas_call(

time: 46.7 us -> 45.8 us (0.981)
  Pallas kernels: 45.2 us -> 44.3 us
    pallas_call x1, Pallas kernels: 45.2 us -> 44.3 us  [adasum(): pl.pallas_call(kernel, out_shape=jax.ShapeDtypeStruct((9, ROWS, LANES), F...]
where the time goes in v4:
time: 45.8 us; the launch traced here: 45.7 us
  Pallas kernels  44.3 us (97%)
  other arithmetic  0.68 us (1%)
  between operations  0.67 us (1%)
    pallas_call x1, Pallas kernels, adasum(): pl.pallas_call(kernel, out_shape=jax.ShapeDtypeStruct((9, ROWS, LANES), F...  44.3 us

profile of v4, /device:TPU:1, one launch (start us, length us, event | category | flops | bytes accessed | tf_op | source)
XLA Modules:
  0.0 45.7 jit_solution(16995777090577818852)
XLA Ops:
  0.6 0.0 copy-start.1
  0.6 0.0 copy-start
  0.7 44.3 %adasum.1 = f32[9,16,128]{2,1,0:T(8,128)S(1)} custom-call(bf16[8,1024,512]{2,1,0:T(8,128)(2,1)} %bitcast.6, bf16[8,1024,128]{2,1,0:T(8,128)(2,1)} %bitcast.7), custom_call_target="tpu_custom_call" | custom-call | tf_op jit(solution)/shard_map/adasum/pallas_call | solution.py:357
  45.0 0.0 copy-done.1
  45.0 0.0 copy-done
  45.0 0.7 %multiply_subtract_fusion = (f32[16,3,3,128]{3,0,2,1:T(8,128)}, f32[16,3,3,128]{3,0,2,1:T(8,128)}) fusion(f32[16,3,3,128]{3,0,2,1:T(8,128)S(1)} %copy-done, f32[16,3,3,128]{3,0,2,1:T(8,128)S(1)} %bitcast.5, f32[16,3,3,128]{3,0,2,1:T(8,128)S(1)} %copy-done.1), kind=kLoop, calls=%fused_computation | loop fusion | flops 73728 | bytes 368640 | tf_op jit(solution)/shard_map/sub | solution.py:374
Async XLA Ops:
  0.6 44.3 %copy-start.1 = (f32[16,3,3,128]{3,0,2,1:T(8,128)S(1)}, f32[16,3,3,128]{3,0,2,1:T(8,128)}, u32[]{:S(2)}) copy-start(f32[16,3,3,128]{3,0,2,1:T(8,128)} %param.7) | copy-start | bytes 221188
  0.6 44.3 %copy-start = (f32[16,3,3,128]{3,0,2,1:T(8,128)S(1)}, f32[16,3,3,128]{3,0,2,1:T(8,128)}, u32[]{:S(2)}) copy-start(f32[16,3,3,128]{3,0,2,1:T(8,128)} %param.6) | copy-start | bytes 221188

commit v5 on v4

--- a/solution.py
+++ b/solution.py
@@ -215,7 +215,7 @@
                 carry[2] + fold(theirs * theirs),
             )
 
-        return lax.fori_loop(0, CHIPS, body, sums, unroll=4)
+        return lax.fori_loop(0, CHIPS, body, sums, unroll=8)
 
     zero = jnp.zeros((8, LANES), F32)
     sums = (zero, zero, zero)

time: 45.8 us -> 45.8 us (level)
  no operation moved by 1% of the time
where the time goes in v5:
time: 45.8 us; the launch traced here: 45.7 us
  Pallas kernels  44.3 us (97%)
  other arithmetic  0.68 us (1%)
  between operations  0.67 us (1%)
    pallas_call x1, Pallas kernels, adasum(): pl.pallas_call(kernel, out_shape=jax.ShapeDtypeStruct((9, ROWS, LANES), F...  44.3 us

profile of v5, /device:TPU:1, one launch (start us, length us, event | category | flops | bytes accessed | tf_op | source)
XLA Modules:
  0.0 45.7 jit_solution(2187788124686819838)
XLA Ops:
  0.6 0.0 copy-start.1
  0.6 0.0 copy-start
  0.7 44.3 %adasum.1 = f32[9,16,128]{2,1,0:T(8,128)S(1)} custom-call(bf16[8,1024,512]{2,1,0:T(8,128)(2,1)} %bitcast.6, bf16[8,1024,128]{2,1,0:T(8,128)(2,1)} %bitcast.7), custom_call_target="tpu_custom_call" | custom-call | tf_op jit(solution)/shard_map/adasum/pallas_call | solution.py:357
  45.0 0.0 copy-done.1
  45.0 0.0 copy-done
  45.0 0.7 %multiply_subtract_fusion = (f32[16,3,3,128]{3,0,2,1:T(8,128)}, f32[16,3,3,128]{3,0,2,1:T(8,128)}) fusion(f32[16,3,3,128]{3,0,2,1:T(8,128)S(1)} %copy-done, f32[16,3,3,128]{3,0,2,1:T(8,128)S(1)} %bitcast.5, f32[16,3,3,128]{3,0,2,1:T(8,128)S(1)} %copy-done.1), kind=kLoop, calls=%fused_computation | loop fusion | flops 73728 | bytes 368640 | tf_op jit(solution)/shard_map/sub | solution.py:374
Async XLA Ops:
  0.6 44.3 %copy-start.1 = (f32[16,3,3,128]{3,0,2,1:T(8,128)S(1)}, f32[16,3,3,128]{3,0,2,1:T(8,128)}, u32[]{:S(2)}) copy-start(f32[16,3,3,128]{3,0,2,1:T(8,128)} %param.7) | copy-start | bytes 221188
  0.6 44.3 %copy-start = (f32[16,3,3,128]{3,0,2,1:T(8,128)S(1)}, f32[16,3,3,128]{3,0,2,1:T(8,128)}, u32[]{:S(2)}) copy-start(f32[16,3,3,128]{3,0,2,1:T(8,128)} %param.6) | copy-start | bytes 221188
